TPU v7x, 512 devices: a whole 4x4x16 slice. The times are simulated.
512 devices in a mesh: mem: 32 (over x_hi, z), gx: 4 (over x_lo, core), gy: 4 (over y).
Axes of the slice: x: 4 (x_hi: 2, x_lo: 2; x = x_hi * 2 + x_lo), y: 4, z: 16, core: 2. Of those that a mesh axis runs over, the one named last changes fastest.
Arguments:
- control: float32 [64, 1024, 1024], P('mem', 'gx', 'gy'), may hold values from -6 to 6
- ensemble: bfloat16 [64, 1024, 1024], P('mem', 'gx', 'gy'), may hold values from -0.75 to 0.75
- obs_index: int32 [1024, 256], P('gx', 'gy'), may hold values from 0 to 255
- obs_value: float32 [1024, 256], P('gx', 'gy'), may hold values from -12 to 12
- obs_weight: float32 [1024, 256], P('gx', 'gy'), may hold values from 1 to 16
Outputs:
- gradient: float32 [64, 1024, 1024], P('mem', 'gx', 'gy')
Inputs may be any that keep to these rules, and one draw needn't show every extreme that they name: obs_index[r, j] is a column inside the y tile j // 64; several observations may share a cell.
All inputs are finite; a program needn't handle non-finite values.
Results may differ from a plain program's by a relative error of at most 0.0003.
Values sent between devices are 32-bit elements; how exact they have to be, the bound alone decides.
A program may use at most 64 MiB of HBM per device.

v0:
```python
import math
import jax
import jax.numpy as jnp
from jax import lax
from jax.sharding import PartitionSpec as P

LEN = 400
saturation = 1.5
highest = lax.Precision.HIGHEST


def from_behind(value, axis, steps):
    count = lax.axis_size(axis)
    leading, last = (max(0, -steps), min(count, count - steps))
    return lax.ppermute(value, axis, [(source, source + steps) for source in range(leading, last)])


def pair_scale():
    decay_rate = math.exp(-1.0 / LEN)
    return (1.0 - decay_rate * decay_rate) / (1.0 + decay_rate * decay_rate)


def filter_tables(length):
    decay_log = -1.0 / LEN
    unit_gain = math.sqrt(1.0 - math.exp(2.0 * decay_log))
    positions = jnp.arange(length, dtype=jnp.float32)
    offsets = positions[:, None] - positions[None, :]
    forward_matrix = jnp.where(
        offsets >= 0, unit_gain * jnp.exp(jnp.maximum(offsets, 0.0) * decay_log), 0.0
    )
    carry_weights = jnp.exp((positions + 1.0) * decay_log)
    chain_factor = jnp.float32(math.exp(length * decay_log))
    return (forward_matrix, carry_weights, chain_factor)


def sweep_x_forward(grid_field):
    forward_matrix, carry_weights, chain_factor = filter_tables(grid_field.shape[1])
    boundary = jnp.einsum("j,mjc->mc", forward_matrix[-1], grid_field, precision=highest)
    local_part = jnp.einsum("ij,mjc->mic", forward_matrix, grid_field, precision=highest)
    incoming = jnp.zeros_like(boundary)
    for repeat in range(lax.axis_size("gx") - 1):
        incoming = from_behind(chain_factor * incoming + boundary, "gx", 1)
    return local_part + carry_weights[None, :, None] * incoming[:, None, :]


def sweep_x_backward(grid_field):
    forward_matrix, carry_weights, chain_factor = filter_tables(grid_field.shape[1])
    boundary = jnp.einsum("j,mjc->mc", forward_matrix[:, 0], grid_field, precision=highest)
    local_part = jnp.einsum("ji,mjc->mic", forward_matrix, grid_field, precision=highest)
    incoming = jnp.zeros_like(boundary)
    for repeat in range(lax.axis_size("gx") - 1):
        incoming = from_behind(chain_factor * incoming + boundary, "gx", -1)
    return local_part + carry_weights[::-1][None, :, None] * incoming[:, None, :]


def sweep_y_forward(grid_field):
    forward_matrix, carry_weights, chain_factor = filter_tables(grid_field.shape[2])
    boundary = jnp.einsum("mrj,j->mr", grid_field, forward_matrix[-1], precision=highest)
    local_part = jnp.einsum("mrj,ij->mri", grid_field, forward_matrix, precision=highest)
    incoming = jnp.zeros_like(boundary)
    for repeat in range(lax.axis_size("gy") - 1):
        incoming = from_behind(chain_factor * incoming + boundary, "gy", 1)
    return local_part + incoming[:, :, None] * carry_weights[None, None, :]


def sweep_y_backward(grid_field):
    forward_matrix, carry_weights, chain_factor = filter_tables(grid_field.shape[2])
    boundary = jnp.einsum("mrj,j->mr", grid_field, forward_matrix[:, 0], precision=highest)
    local_part = jnp.einsum("mrj,ji->mri", grid_field, forward_matrix, precision=highest)
    incoming = jnp.zeros_like(boundary)
    for repeat in range(lax.axis_size("gy") - 1):
        incoming = from_behind(chain_factor * incoming + boundary, "gy", -1)
    return local_part + incoming[:, :, None] * carry_weights[::-1][None, None, :]


def smooth(grid_field):
    along_x = sweep_x_backward(sweep_x_forward(grid_field))
    return pair_scale() * sweep_y_backward(sweep_y_forward(along_x))


def smooth_adjoint(grid_field):
    along_y = sweep_y_backward(sweep_y_forward(grid_field))
    return pair_scale() * sweep_x_backward(sweep_x_forward(along_y))


def obs_residual(grid_field, columns, values, weights):
    picked = jnp.take_along_axis(grid_field, columns, axis=1)
    misfit = picked - values
    return weights * saturation * jnp.tanh(misfit / saturation)


def place_residual(residual, columns, like_field):
    row_ids = lax.broadcasted_iota(jnp.int32, columns.shape, 0)
    return jnp.zeros_like(like_field).at[row_ids, columns].add(residual)


def on_device(control, ensemble, obs_index, obs_value, obs_weight):
    smoothed = smooth(control)
    partial_value = jnp.sum(ensemble * smoothed, axis=0)
    increment = lax.psum(partial_value, "mem")
    forcing = place_residual(
        obs_residual(increment, obs_index, obs_value, obs_weight), obs_index, increment
    )
    adjoint = smooth_adjoint(ensemble * forcing[None])
    return control + adjoint


def solution(mesh):
    return jax.shard_map(
        on_device,
        mesh=mesh,
        in_specs=(
            P("mem", "gx", "gy"),
            P("mem", "gx", "gy"),
            P("gx", "gy"),
            P("gx", "gy"),
            P("gx", "gy"),
        ),
        out_specs=P("mem", "gx", "gy"),
        check_vma=False,
    )
```

profile of v0, /device:TPU:1, one launch (start us, length us, event | category | flops | bytes accessed | tf_op | source)
XLA Modules:
  0.0 676.7 jit_solution(3496676984004328318)
XLA Ops:
  8.2 4.5 collective-permute-start
  12.7 4.3 collective-permute-done
  20.1 3.8 collective-permute-start.2
  26.9 3.5 collective-permute-done.3
  32.4 3.0 collective-permute-done.4
  37.4 2.9 collective-permute-done.5
  44.4 3.6 collective-permute-start.7
  48.7 3.7 collective-permute-start.8
  55.4 3.0 collective-permute-done.9
  59.7 3.0 collective-permute-done.10
  64.2 2.9 collective-permute-done.11
  69.3 289.4 %all-reduce.2.cloned.1.call-done = f32[256,256]{1,0:T(8,128)} async-done(((f32[256,256]{1,0:T(8,128)}), f32[256,256]{1,0:T(8,128)}) %all-reduce.2.cloned.1.call-update) | async-done | bytes 262160 | tf_op jit(solution)/shard_map/psum | solution.py:100
  358.8 109.0 %gather_fusion = f32[16384]{0:T(1024)S(1)} fusion(f32[256,256]{1,0:T(8,128)} %all-reduce.2.cloned.1.call-done, s32[16384]{0:T(1024)S(1)} %reshape.46), kind=kCustom, calls=%fused_computation | custom fusion | bytes 262144 | tf_op jit(solution)/shard_map/jit(take_along_axis)/gather | solution.py:87
  468.2 113.5 %scatter_custom_fusion = f32[65536]{0:T(1024)S(1)} fusion(s32[16384]{0:T(1024)S(1)} %reshape.52, f32[16384]{0:T(1024)S(1)} %reshape.54, f32[]{:T(128)} %constant.12.clone.1), kind=kCustom, calls=%fused_computation.52 | custom fusion | flops 16384 | bytes 262148
  582.4 3.1 collective-permute-start.12
  586.2 3.6 collective-permute-start.13
  590.5 3.6 collective-permute-start.14
  597.1 3.0 collective-permute-done.15
  601.5 3.0 collective-permute-done.16
  610.1 30.8 %collective-permute-start.18 = (f32[2,256]{1,0:T(2,128)S(1)}, f32[2,256]{1,0:T(2,128)S(1)}, u32[]{:S(2)}, u32[]{:S(2)}) collective-permute-start(f32[2,256]{1,0:T(2,128)S(1)} %bitcast.136), channel_id=1, source_target_pairs={{0,4},{4,8},{8,12},{1,5},{5,9},{9,13},{2,6},{6,10},{10,14},{3,7},{... | collective-permute-start | bytes 6152 | tf_op jit(solution)/shard_map/ppermute | solution.py:15
  641.7 4.2 collective-permute-start.19
  646.6 4.2 collective-permute-start.20
  654.5 3.5 collective-permute-done.21
  660.0 3.0 collective-permute-done.22
  (106 shorter events, 50.8 us)
Async XLA Ops:
  6.5 352.2 %all-reduce.2.cloned.1.call-start = ((), (), s32[]{:S(2)}) async-start(), calls=%async_computation | async-start | bytes 524288 | tf_op jit(solution)/shard_map/psum | solution.py:100
  8.2 8.8 %collective-permute-start = (f32[2,256]{1,0:T(2,128)S(1)}, f32[2,256]{1,0:T(2,128)S(1)}, u32[]{:S(2)}, u32[]{:S(2)}) collective-permute-start(f32[2,256]{1,0:T(2,128)S(1)} %bitcast.130), channel_id=1, source_target_pairs={{0,4},{4,8},{8,12},{1,5},{5,9},{9,13},{2,6},{6,10},{10,14},{3,7},{... | collective-permute-start | bytes 6152 | tf_op jit(solution)/shard_map/ppermute | solution.py:15
  17.0 3.0 collective-permute-start.1
  20.1 4.5 collective-permute-start.2
  25.0 5.4 collective-permute-start.3
  30.5 4.9 collective-permute-start.4
  35.4 4.9 collective-permute-start.5
  44.4 4.3 collective-permute-start.7
  48.7 4.7 collective-permute-start.8
  54.1 4.3 collective-permute-start.9
  58.4 4.3 collective-permute-start.10
  62.7 4.3 collective-permute-start.11
  582.4 3.8 collective-permute-start.12
  586.2 4.3 collective-permute-start.13
  590.5 4.6 collective-permute-start.14
  595.8 4.3 collective-permute-start.15
  600.2 4.3 collective-permute-start.16
  604.5 4.3 collective-permute-start.17
  610.1 31.6 %collective-permute-start.18 = (f32[2,256]{1,0:T(2,128)S(1)}, f32[2,256]{1,0:T(2,128)S(1)}, u32[]{:S(2)}, u32[]{:S(2)}) collective-permute-start(f32[2,256]{1,0:T(2,128)S(1)} %bitcast.136), channel_id=1, source_target_pairs={{0,4},{4,8},{8,12},{1,5},{5,9},{9,13},{2,6},{6,10},{10,14},{3,7},{... | collective-permute-start | bytes 6152 | tf_op jit(solution)/shard_map/ppermute | solution.py:15
  641.7 4.9 collective-permute-start.19
  646.6 4.9 collective-permute-start.20
  652.6 5.4 collective-permute-start.21
  658.1 4.9 collective-permute-start.22
  663.0 4.9 collective-permute-start.23
  (7 other events, 830.2 us)
Sparse Core Ops, SparseCore 0:
  68.9 289.8 all-reduce.1
where the time goes:
time: 677 us
  waiting for transfers between devices  336 us (50%)
  other arithmetic  114 us (17%)
  local copies, waits for them, and re-layouts  112 us (17%)
  starting transfers between devices  88.2 us (13%)
  between operations  13.9 us (2%)
  matrix products  12.1 us (2%)
    psum x1, waiting for transfers between devices, on_device(): increment = lax.psum(partial_value, 'mem')  289 us
    unnamed x4, other arithmetic  114 us
    gather x3, local copies, waits for them, and re-layouts, obs_residual(): picked = jnp.take_along_axis(grid_field, columns, axis=1)  109 us
    ppermute x24, starting transfers between devices, from_behind(): lax.ppermute(value, axis, [(source, source + steps) for source in range(l...  88.2 us
    ppermute x24, waiting for transfers between devices, from_behind(): lax.ppermute(value, axis, [(source, source + steps) for source in range(l...  46.8 us
  transfers between devices with their start and end apart: 25, of which 23 were waited for; matrix products, arithmetic and copies ran while one was open for 1% of the time, Pallas kernels for 0%

commit v1 on v0

--- a/solution.py
+++ b/solution.py
@@ -3,6 +3,7 @@
 import jax.numpy as jnp
 from jax import lax
 from jax.sharding import PartitionSpec as P
+from jax.lax import all_gather
 
 LEN = 400
 saturation = 1.5
@@ -97,7 +98,7 @@
 def on_device(control, ensemble, obs_index, obs_value, obs_weight):
     smoothed = smooth(control)
     partial_value = jnp.sum(ensemble * smoothed, axis=0)
-    increment = lax.psum(partial_value, "mem")
+    increment = jnp.sum(all_gather(partial_value, axis_name="mem"), 0)
     forcing = place_residual(
         obs_residual(increment, obs_index, obs_value, obs_weight), obs_index, increment
     )

time: 677 us -> 616 us (0.910)
  waiting for transfers between devices: 336 us -> 253 us
  local copies, waits for them, and re-layouts: 112 us -> 141 us
  starting transfers between devices: 88.2 us -> 76.7 us
    psum x1 -> x0, waiting for transfers between devices: 289 us -> none  [on_device(): increment = lax.psum(partial_value, 'mem')]
    all_gather x0 -> x1, waiting for transfers between devices: none -> 207 us  [on_device(): increment = jnp.sum(all_gather(partial_value, axis_name='mem'), 0)]
    gather x3, local copies, waits for them, and re-layouts: 109 us -> 131 us  [obs_residual(): picked = jnp.take_along_axis(grid_field, columns, axis=1)]
    ppermute x24, starting transfers between devices: 88.2 us -> 76.7 us  [from_behind(): lax.ppermute(value, axis, [(source, source + steps) for source in range(l...]
    unnamed x16 -> x15, local copies, waits for them, and re-layouts: 0.54 us -> 8.31 us
  transfers between devices with their start and end apart: 25 -> 25, of which waited for: 23 -> 22; matrix products, arithmetic and copies ran while one was open for 1% -> 1% of each run, Pallas kernels for 0% -> 0%
where the time goes in v1:
time: 616 us; the launch traced here: 615 us
  waiting for transfers between devices  253 us (41%)
  local copies, waits for them, and re-layouts  141 us (23%)
  other arithmetic  117 us (19%)
  starting transfers between devices  76.7 us (12%)
  between operations  13.9 us (2%)
  matrix products  13.8 us (2%)
    all_gather x1, waiting for transfers between devices, on_device(): increment = jnp.sum(all_gather(partial_value, axis_name='mem'), 0)  207 us
    gather x3, local copies, waits for them, and re-layouts, obs_residual(): picked = jnp.take_along_axis(grid_field, columns, axis=1)  131 us
    unnamed x4, other arithmetic  114 us
    ppermute x24, starting transfers between devices, from_behind(): lax.ppermute(value, axis, [(source, source + steps) for source in range(l...  76.7 us
    ppermute x24, waiting for transfers between devices, from_behind(): lax.ppermute(value, axis, [(source, source + steps) for source in range(l...  45.3 us
  transfers between devices with their start and end apart: 25, of which 22 were waited for; matrix products, arithmetic and copies ran while one was open for 1% of the time, Pallas kernels for 0%

profile of v1, /device:TPU:1, one launch (start us, length us, event | category | flops | bytes accessed | tf_op | source)
XLA Modules:
  0.0 614.8 jit_solution(8912696445347619953)
XLA Ops:
  8.2 4.5 collective-permute-start
  12.7 4.3 collective-permute-done
  20.7 3.1 collective-permute-start.2
  26.9 3.5 collective-permute-done.3
  32.4 3.0 collective-permute-done.4
  44.4 3.6 collective-permute-start.7
  48.7 3.7 collective-permute-start.8
  55.3 3.0 collective-permute-done.9
  59.7 3.0 collective-permute-done.10
  70.0 207.5 %all-gather.3.cloned.1.call-done = f32[8192,256]{0,1:T(8,128)} async-done(((f32[256,256]{0,1:T(8,128)}), f32[8192,256]{0,1:T(8,128)}) %all-gather.3.cloned.1.call-update) | async-done | bytes 8388624 | tf_op jit(solution)/shard_map/all_gather | solution.py:101
  277.5 6.8 %copy.213 = f32[32,8,32,256]{3,2,1,0:T(8,128)S(1)} copy(f32[32,8,32,256]{3,1,2,0:T(8,128)} %bitcast.131) | data formatting | bytes 16777216
  286.3 130.6 %gather_fusion = f32[16384]{0:T(1024)S(1)} fusion(f32[256,256]{0,1:T(8,128)S(1)} %bitcast_reduce_fusion, s32[16384]{0:T(1024)S(1)} %reshape.46), kind=kCustom, calls=%fused_computation | custom fusion | bytes 262144 | tf_op jit(solution)/shard_map/jit(take_along_axis)/gather | solution.py:88
  417.3 113.5 %scatter_custom_fusion = f32[65536]{0:T(1024)S(1)} fusion(s32[16384]{0:T(1024)S(1)} %reshape.52, f32[16384]{0:T(1024)S(1)} %reshape.54, f32[]{:T(128)} %constant.12.clone.1), kind=kCustom, calls=%fused_computation.53 | custom fusion | flops 16384 | bytes 262148
  531.5 3.1 collective-permute-start.12
  535.3 3.6 collective-permute-start.13
  539.6 3.6 collective-permute-start.14
  546.2 3.0 collective-permute-done.15
  550.6 3.0 collective-permute-done.16
  554.9 3.0 collective-permute-done.17
  559.2 19.8 %collective-permute-start.18 = (f32[2,256]{1,0:T(2,128)S(1)}, f32[2,256]{1,0:T(2,128)S(1)}, u32[]{:S(2)}, u32[]{:S(2)}) collective-permute-start(f32[2,256]{1,0:T(2,128)S(1)} %bitcast.142), channel_id=1, source_target_pairs={{0,4},{4,8},{8,12},{1,5},{5,9},{9,13},{2,6},{6,10},{10,14},{3,7},{... | collective-permute-start | bytes 6152 | tf_op jit(solution)/shard_map/ppermute | solution.py:16
  579.8 4.2 collective-permute-start.19
  584.7 4.4 collective-permute-start.20
  592.6 3.5 collective-permute-done.21
  598.0 3.0 collective-permute-done.22
  (105 shorter events, 56.6 us)
Async XLA Ops:
  6.5 271.0 %all-gather.3.cloned.1.call-start = ((), (), s32[]{:S(2)}) async-start(), calls=%async_computation | async-start | bytes 8650752 | tf_op jit(solution)/shard_map/all_gather | solution.py:101
  8.2 8.8 %collective-permute-start = (f32[2,256]{1,0:T(2,128)S(1)}, f32[2,256]{1,0:T(2,128)S(1)}, u32[]{:S(2)}, u32[]{:S(2)}) collective-permute-start(f32[2,256]{1,0:T(2,128)S(1)} %bitcast.136), channel_id=1, source_target_pairs={{0,4},{4,8},{8,12},{1,5},{5,9},{9,13},{2,6},{6,10},{10,14},{3,7},{... | collective-permute-start | bytes 6152 | tf_op jit(solution)/shard_map/ppermute | solution.py:16
  17.0 3.7 collective-permute-start.1
  20.7 3.8 collective-permute-start.2
  25.0 5.4 collective-permute-start.3
  30.5 4.9 collective-permute-start.4
  35.4 4.9 collective-permute-start.5
  44.4 4.3 collective-permute-start.7
  48.7 4.7 collective-permute-start.8
  54.0 4.3 collective-permute-start.9
  58.4 4.3 collective-permute-start.10
  62.7 4.3 collective-permute-start.11
  531.5 3.8 collective-permute-start.12
  535.3 4.3 collective-permute-start.13
  539.6 4.6 collective-permute-start.14
  544.9 4.3 collective-permute-start.15
  549.3 4.3 collective-permute-start.16
  553.6 4.3 collective-permute-start.17
  559.2 20.5 %collective-permute-start.18 = (f32[2,256]{1,0:T(2,128)S(1)}, f32[2,256]{1,0:T(2,128)S(1)}, u32[]{:S(2)}, u32[]{:S(2)}) collective-permute-start(f32[2,256]{1,0:T(2,128)S(1)} %bitcast.142), channel_id=1, source_target_pairs={{0,4},{4,8},{8,12},{1,5},{5,9},{9,13},{2,6},{6,10},{10,14},{3,7},{... | collective-permute-start | bytes 6152 | tf_op jit(solution)/shard_map/ppermute | solution.py:16
  579.8 4.9 collective-permute-start.19
  584.7 4.9 collective-permute-start.20
  590.7 5.4 collective-permute-start.21
  596.1 4.9 collective-permute-start.22
  601.0 4.9 collective-permute-start.23
  (6 other events, 707.1 us)
Sparse Core Ops, SparseCore 0:
  68.7 208.7 all-gather.2
